TPU v7x, 512 devices: a whole 4x8x8 slice. The times are simulated.
512 devices in a mesh: term: 8 (over z), sector: 64 (over x, y, core).
Axes of the slice: x: 4, y: 8, z: 8, core: 2. Of those that a mesh axis runs over, the one named last changes fastest.
Arguments:
- wave_tiles: bfloat16 [1024, 2, 128, 128], P('sector'), may hold values from -6 to 6
- left_env: bfloat16 [8, 64, 128, 128], P('term', 'sector'), may hold values from -0.5 to 0.5
- right_env: bfloat16 [8, 64, 128, 128], P('term', 'sector'), may hold values from -0.5 to 0.5
- send_list: int32 [64, 128], P('sector'), may hold values from -1 to 15, as said below
- left_tasks: int32 [8, 64, 96, 3], P('term', 'sector'), may hold values from 0 to 127, as said below
- right_tasks: int32 [8, 64, 256, 3], P('term', 'sector'), may hold values from 0 to 63, as said below
Outputs:
- sigma: float32 [1024, 2, 128, 128], P('sector', None, 'term')
Inputs may be any that keep to these rules, and one draw needn't show every extreme that they name: send_list[s, o * 2 + c] is a tile index local to sender s, or -1 for an empty slot; some owner drawn from the seed receives a full 2 tiles from every sender. `left_tasks`: entries 0, 1, 2 lie below 64, 128 and 32. `right_tasks`: entries 0, 1, 2 lie below 32, 64 and 16.
All inputs are finite; a program needn't handle non-finite values.
Results may differ from a plain program's by a relative error of at most 0.0029.
Values may be sent and summed in bfloat16 or wider, within the bound.
A program may use at most 128 MiB of HBM per device.

v0:
```python
import math
import jax
import jax.numpy as jnp
from jax import lax
from jax.sharding import PartitionSpec as P

INTER_TILES = 32


def run_tasks(tasks, first_tiles, second_tiles, contract, count):
    block = math.gcd(tasks.shape[0], 32)
    shape = (count,) + tuple(contract(first_tiles[:1], second_tiles[:1]).shape[1:])

    def step(turn, total):
        rows = lax.dynamic_slice_in_dim(tasks, turn * block, block, 0)
        first = jnp.take(first_tiles, rows[:, 0], axis=0)
        second = jnp.take(second_tiles, rows[:, 1], axis=0)
        return total.at[rows[:, 2]].add(contract(first, second))

    return lax.fori_loop(0, tasks.shape[0] // block, step, jnp.zeros(shape, jnp.float32))


def left_product(env_part, wave_part):
    return jnp.einsum("bij,bvjk->bvik", env_part, wave_part, preferred_element_type=jnp.float32)


def right_product(inter_part, env_part):
    return jnp.einsum("bvij,bjk->bvik", inter_part, env_part, preferred_element_type=jnp.float32)


def shards(wave_tiles, left_env, right_env, send_list, left_tasks, right_tasks):
    env_left, env_right = (
        lax.all_gather(left_env, "sector", axis=1, tiled=True),
        lax.all_gather(right_env, "sector", axis=1, tiled=True),
    )
    env_left = env_left[0]
    env_right = env_right[0]
    slot_list = send_list[0]
    live = slot_list >= 0
    picked = jnp.take(wave_tiles, jnp.maximum(slot_list, 0), axis=0)
    outgoing = jnp.where(live[:, None, None, None], picked, jnp.zeros((), jnp.bfloat16))
    tile_dim = wave_tiles.shape[2]
    groups = lax.axis_size("term")
    share = tile_dim // groups
    received = lax.all_to_all(outgoing, "sector", split_axis=0, concat_axis=0, tiled=True)
    inter = run_tasks(left_tasks[0, 0], env_left, received, left_product, INTER_TILES).astype(
        jnp.bfloat16
    )
    partial_value = run_tasks(
        right_tasks[0, 0], inter, env_right, right_product, wave_tiles.shape[0]
    )
    summed = lax.psum(partial_value, "term")
    return lax.dynamic_slice_in_dim(summed, lax.axis_index("term") * share, share, 2)


def solution(mesh):
    in_specs = (
        P("sector", None, None, None),
        P("term", "sector", None, None),
        P("term", "sector", None, None),
        P("sector", None),
        P("term", "sector", None, None),
        P("term", "sector", None, None),
    )
    out_specs = P("sector", None, "term", None)
    return jax.shard_map(shards, mesh=mesh, in_specs=in_specs, out_specs=out_specs, check_vma=False)
```

profile of v0, /device:TPU:2, one launch (start us, length us, event | category | flops | bytes accessed | tf_op | source)
XLA Modules:
  0.0 562.8 jit_solution(14975568767976974510)
XLA Ops:
  8.0 6.5 %gather_fusion.4 = bf16[128,2,128,128]{3,2,1,0:T(8,128)(2,1)} fusion(bf16[16,2,128,128]{3,2,1,0:T(8,128)(2,1)S(1)} %copy-done, s32[1024]{0:T(1024)S(1)} %pad_clamp_fusion.4), kind=kCustom, calls=%fused_computation.4 | custom fusion | bytes 16777728 | tf_op jit(solution)/shard_map/jit(_take)/gather | solution.py:40
  14.5 7.5 %select_select_fusion = bf16[128,2,128,128]{3,2,1,0:T(8,128)(2,1)} fusion(bf16[128,2,128,128]{3,2,1,0:T(8,128)(2,1)} %gather_fusion.4, pred[128]{0:T(512)(128)(4,1)S(1)} %get-tuple-element.225, pred[128]{0:T(512)(128)(4,1)S(1)} %get-tuple-element.224), kind=kLoop, calls=%fused_computation.45 | loop fusion | flops 8388608 | bytes 16777472 | tf_op jit(solution)/shard_map/jit(_where)/select_n | solution.py:41
  22.0 11.3 %all-to-all-start = ((bf16[128,2,128,128]{3,2,1,0:T(8,128)(2,1)}), bf16[128,2,128,128]{3,2,1,0:T(8,128)(2,1)}, u32[]{:S(2)}, u32[]{:S(2)}) async-start(bf16[128,2,128,128]{3,2,1,0:T(8,128)(2,1)} %select_select_fusion), calls=%async_computation | async-start | bytes 16777216 | tf_op jit(solution)/shard_map/all_to_all | solution.py:45
  34.8 102.3 %all-gather.3.cloned.1.call-done = bf16[1,64,128,128]{3,2,0,1:T(8,128)(2,1)} async-done(((bf16[1,1,128,128]{3,2,0,1:T(8,128)(2,1)}), bf16[1,64,128,128]{3,2,0,1:T(8,128)(2,1)}) %all-gather.3.cloned.1.call-update) | async-done | bytes 2097168 | tf_op jit(solution)/shard_map/all_gather | solution.py:33
  137.1 90.6 %all-to-all-done = bf16[128,2,128,128]{3,2,1,0:T(8,128)(2,1)} async-done(((bf16[128,2,128,128]{3,2,1,0:T(8,128)(2,1)}), bf16[128,2,128,128]{3,2,1,0:T(8,128)(2,1)}, u32[]{:S(2)}, u32[]{:S(2)}) %all-to-all-start) | async-done | bytes 8388640 | tf_op jit(solution)/shard_map/all_to_all | solution.py:45
  230.2 82.3 %while.26 = (s32[]{:T(128)}, f32[32,2,128,128]{3,2,1,0:T(8,128)}, s32[96,3]{0,1:T(4,128)S(1)}, bf16[128,2,128,128]{3,2,1,0:T(8,128)(2,1)}, bf16[64,128,128]{2,1,...) while((s32[]{:T(128)}, f32[32,2,128,128]{3,2,1,0:T(8,128)}, s32[96,3]{0,1:T(4,128)S(1)}, ...), condition=%wide.region_2.4_spmd, body=%wide.region_0.3_spmd.sunk | while | flops 271059520 | bytes 34613776 | solution.py:20
  230.3 4.4 gather_fusion
  234.7 3.4 gather_fusion.1
  238.1 4.0 convolution_bitcast_fusion.2
  242.1 5.6 copy.23
  247.7 10.1 %scatter_fusion = f32[32,2,128,128]{3,2,1,0:T(8,128)} fusion(f32[32,2,128,128]{3,2,1,0:T(8,128)} %get-tuple-element.314, s32[32]{0:T(128)S(1)} %get-tuple-element.291, f32[32,2,128,128]{3,2,1,0:T(8,128)} %copy.23), kind=kCustom, calls=%fused_computation.5.clone.1 | custom fusion | flops 1048576 | bytes 12583040 | tf_op jit(solution)/shard_map/while/body/eval_jaxpr/scatter-add | solution.py:18
  257.9 4.3 gather_fusion
  262.2 3.3 gather_fusion.1
  265.6 4.0 convolution_bitcast_fusion.2
  269.6 5.6 copy.23
  275.2 9.9 %scatter_fusion = f32[32,2,128,128]{3,2,1,0:T(8,128)} fusion(f32[32,2,128,128]{3,2,1,0:T(8,128)} %get-tuple-element.314, s32[32]{0:T(128)S(1)} %get-tuple-element.291, f32[32,2,128,128]{3,2,1,0:T(8,128)} %copy.23), kind=kCustom, calls=%fused_computation.5.clone.1 | custom fusion | flops 1048576 | bytes 12583040 | tf_op jit(solution)/shard_map/while/body/eval_jaxpr/scatter-add | solution.py:18
  285.2 4.3 gather_fusion
  289.6 3.3 gather_fusion.1
  292.9 4.0 convolution_bitcast_fusion.2
  296.9 5.6 copy.23
  302.6 9.9 %scatter_fusion = f32[32,2,128,128]{3,2,1,0:T(8,128)} fusion(f32[32,2,128,128]{3,2,1,0:T(8,128)} %get-tuple-element.314, s32[32]{0:T(128)S(1)} %get-tuple-element.291, f32[32,2,128,128]{3,2,1,0:T(8,128)} %copy.23), kind=kCustom, calls=%fused_computation.5.clone.1 | custom fusion | flops 1048576 | bytes 12583040 | tf_op jit(solution)/shard_map/while/body/eval_jaxpr/scatter-add | solution.py:18
  312.5 3.9 convert_element_type.3
  316.6 145.3 %while.27 = (s32[]{:T(128)}, f32[16,2,128,128]{3,2,1,0:T(8,128)S(1)}, s32[256,3]{0,1:T(4,128)S(1)}, bf16[32,2,128,128]{3,2,1,0:T(8,128)(2,1)}, bf16[64,128,128]{...) while((s32[]{:T(128)}, f32[16,2,128,128]{3,2,1,0:T(8,128)S(1)}, ...), condition=%wide.region_5.7_spmd, body=%wide.region_3.6_spmd.sunk | while | flops 271059520 | bytes 26225168 | solution.py:20
  316.7 3.7 gather_fusion.2
  323.7 4.6 fusion.34
  328.3 6.5 %scatter_fusion.1 = f32[16,2,128,128]{3,2,1,0:T(8,128)S(1)} fusion(f32[16,2,128,128]{3,2,1,0:T(8,128)S(1)} %get-tuple-element.341, s32[32]{0:T(128)S(1)} %get-tuple-element.300, f32[32,2,128,128]{3,2,1,0:T(8,128)} %fusion.34), kind=kCustom, calls=%fused_computation.6.clone.1 | custom fusion | flops 1048576 | bytes 12583040 | tf_op jit(solution)/shard_map/while/body/eval_jaxpr/scatter-add | solution.py:18
  334.9 3.7 gather_fusion.2
  341.9 4.6 fusion.34
  346.5 6.5 %scatter_fusion.1 = f32[16,2,128,128]{3,2,1,0:T(8,128)S(1)} fusion(f32[16,2,128,128]{3,2,1,0:T(8,128)S(1)} %get-tuple-element.341, s32[32]{0:T(128)S(1)} %get-tuple-element.300, f32[32,2,128,128]{3,2,1,0:T(8,128)} %fusion.34), kind=kCustom, calls=%fused_computation.6.clone.1 | custom fusion | flops 1048576 | bytes 12583040 | tf_op jit(solution)/shard_map/while/body/eval_jaxpr/scatter-add | solution.py:18
  353.1 3.7 gather_fusion.2
  360.0 4.6 fusion.34
  364.6 6.5 %scatter_fusion.1 = f32[16,2,128,128]{3,2,1,0:T(8,128)S(1)} fusion(f32[16,2,128,128]{3,2,1,0:T(8,128)S(1)} %get-tuple-element.341, s32[32]{0:T(128)S(1)} %get-tuple-element.300, f32[32,2,128,128]{3,2,1,0:T(8,128)} %fusion.34), kind=kCustom, calls=%fused_computation.6.clone.1 | custom fusion | flops 1048576 | bytes 12583040 | tf_op jit(solution)/shard_map/while/body/eval_jaxpr/scatter-add | solution.py:18
  371.2 3.7 gather_fusion.2
  378.2 4.6 fusion.34
  382.8 6.5 %scatter_fusion.1 = f32[16,2,128,128]{3,2,1,0:T(8,128)S(1)} fusion(f32[16,2,128,128]{3,2,1,0:T(8,128)S(1)} %get-tuple-element.341, s32[32]{0:T(128)S(1)} %get-tuple-element.300, f32[32,2,128,128]{3,2,1,0:T(8,128)} %fusion.34), kind=kCustom, calls=%fused_computation.6.clone.1 | custom fusion | flops 1048576 | bytes 12583040 | tf_op jit(solution)/shard_map/while/body/eval_jaxpr/scatter-add | solution.py:18
  389.4 3.7 gather_fusion.2
  396.4 4.6 fusion.34
  400.9 6.5 %scatter_fusion.1 = f32[16,2,128,128]{3,2,1,0:T(8,128)S(1)} fusion(f32[16,2,128,128]{3,2,1,0:T(8,128)S(1)} %get-tuple-element.341, s32[32]{0:T(128)S(1)} %get-tuple-element.300, f32[32,2,128,128]{3,2,1,0:T(8,128)} %fusion.34), kind=kCustom, calls=%fused_computation.6.clone.1 | custom fusion | flops 1048576 | bytes 12583040 | tf_op jit(solution)/shard_map/while/body/eval_jaxpr/scatter-add | solution.py:18
  407.5 3.7 gather_fusion.2
  414.5 4.6 fusion.34
  419.1 6.5 %scatter_fusion.1 = f32[16,2,128,128]{3,2,1,0:T(8,128)S(1)} fusion(f32[16,2,128,128]{3,2,1,0:T(8,128)S(1)} %get-tuple-element.341, s32[32]{0:T(128)S(1)} %get-tuple-element.300, f32[32,2,128,128]{3,2,1,0:T(8,128)} %fusion.34), kind=kCustom, calls=%fused_computation.6.clone.1 | custom fusion | flops 1048576 | bytes 12583040 | tf_op jit(solution)/shard_map/while/body/eval_jaxpr/scatter-add | solution.py:18
  425.7 3.7 gather_fusion.2
  432.7 4.6 fusion.34
  437.2 6.5 %scatter_fusion.1 = f32[16,2,128,128]{3,2,1,0:T(8,128)S(1)} fusion(f32[16,2,128,128]{3,2,1,0:T(8,128)S(1)} %get-tuple-element.341, s32[32]{0:T(128)S(1)} %get-tuple-element.300, f32[32,2,128,128]{3,2,1,0:T(8,128)} %fusion.34), kind=kCustom, calls=%fused_computation.6.clone.1 | custom fusion | flops 1048576 | bytes 12583040 | tf_op jit(solution)/shard_map/while/body/eval_jaxpr/scatter-add | solution.py:18
  443.8 3.7 gather_fusion.2
  450.8 4.6 fusion.34
  455.4 6.5 %scatter_fusion.1 = f32[16,2,128,128]{3,2,1,0:T(8,128)S(1)} fusion(f32[16,2,128,128]{3,2,1,0:T(8,128)S(1)} %get-tuple-element.341, s32[32]{0:T(128)S(1)} %get-tuple-element.300, f32[32,2,128,128]{3,2,1,0:T(8,128)} %fusion.34), kind=kCustom, calls=%fused_computation.6.clone.1 | custom fusion | flops 1048576 | bytes 12583040 | tf_op jit(solution)/shard_map/while/body/eval_jaxpr/scatter-add | solution.py:18
  463.2 91.4 %all-reduce.2.cloned.1.call-done = f32[16,2,128,128]{3,2,1,0:T(8,128)} async-done(((f32[16,2,128,128]{3,2,1,0:T(8,128)}), f32[16,2,128,128]{3,2,1,0:T(8,128)}) %all-reduce.2.cloned.1.call-update) | async-done | bytes 2097168 | tf_op jit(solution)/shard_map/psum | solution.py:52
  (97 shorter events, 35.7 us)
Async XLA Ops:
  6.5 1.4 copy-start
  22.0 12.8 %copy-start.3 = (s32[1,1,96,3]{2,1,3,0:T(1,128)S(1)}, s32[1,1,96,3]{2,1,3,0:T(1,128)}, u32[]{:S(2)}) copy-start(s32[1,1,96,3]{2,1,3,0:T(1,128)} %param.16) | copy-start | bytes 3460
  22.0 12.8 %copy-start.2 = (s32[1,1,256,3]{2,1,3,0:T(1,128)S(1)}, s32[1,1,256,3]{2,1,3,0:T(1,128)}, u32[]{:S(2)}) copy-start(s32[1,1,256,3]{2,1,3,0:T(1,128)} %param.17) | copy-start | bytes 9220
  22.0 205.8 %all-to-all-start = ((bf16[128,2,128,128]{3,2,1,0:T(8,128)(2,1)}), bf16[128,2,128,128]{3,2,1,0:T(8,128)(2,1)}, u32[]{:S(2)}, u32[]{:S(2)}) async-start(bf16[128,2,128,128]{3,2,1,0:T(8,128)(2,1)} %select_select_fusion), calls=%async_computation | async-start | bytes 16777216 | tf_op jit(solution)/shard_map/all_to_all | solution.py:45
  33.3 103.9 %all-gather.3.cloned.1.call-start = ((), (), s32[]{:S(2)}) async-start(), calls=%async_computation.1 | async-start | bytes 2129920 | tf_op jit(solution)/shard_map/all_gather | solution.py:33
  34.0 282.4 %all-gather.5.cloned.1.call-start = ((), (), s32[]{:S(2)}) async-start(), calls=%async_computation.2 | async-start | bytes 2129920 | tf_op jit(solution)/shard_map/all_gather | solution.py:34
  34.8 519.8 %all-reduce.2.cloned.1.call-start = ((), (), s32[]{:S(2)}) async-start(), calls=%async_computation.3 | async-start | bytes 4194304 | tf_op jit(solution)/shard_map/psum | solution.py:52
  461.9 1.3 copy-start.1
Sparse Core Ops, SparseCore 0:
  37.5 99.6 all-gather.2
  140.5 95.8 all-gather.4
  463.3 91.2 all-reduce.1
where the time goes:
time: 565 us; the launch traced here: 563 us
  waiting for transfers between devices  286 us (51%)
  local copies, waits for them, and re-layouts  109 us (19%)
  other arithmetic  95 us (17%)
  matrix products  48.7 us (9%)
  between operations  13.2 us (2%)
  starting transfers between devices  11.4 us (2%)
    all_gather x1, waiting for transfers between devices, shards(): lax.all_gather(left_env, 'sector', axis=1, tiled=True)  102 us
    psum x1, waiting for transfers between devices, shards(): summed = lax.psum(partial_value, 'term')  91.4 us
    all_to_all x1, waiting for transfers between devices, shards(): lax.all_to_all(outgoing, 'sector', split_axis=0, concat_axis=0, tiled=True)  90.6 us
    scatter-add x11, other arithmetic, step(): return total.at[rows[:, 2]].add(contract(first, second))  81.8 us
    gather x11, local copies, waits for them, and re-layouts, step(): first = jnp.take(first_tiles, rows[:, 0], axis=0)  39.8 us
    gather x11, local copies, waits for them, and re-layouts, step(): second = jnp.take(second_tiles, rows[:, 1], axis=0)  38.9 us
    dot_general x8, matrix products, right_product(): jnp.einsum('bvij,bjk->bvik', inter_part, env_part, preferred_element_type...  36.6 us
    transpose x3, local copies, waits for them, and re-layouts, left_product(): jnp.einsum('bij,bvjk->bvik', env_part, wave_part, preferred_element_type=...  16.9 us
  transfers between devices with their start and end apart: 4, of which 3 were waited for; matrix products, arithmetic and copies ran while one was open for 16% of the time, Pallas kernels for 0%

commit v1 on v0

--- a/solution.py
+++ b/solution.py
@@ -49,7 +49,7 @@
     partial_value = run_tasks(
         right_tasks[0, 0], inter, env_right, right_product, wave_tiles.shape[0]
     )
-    summed = lax.psum(partial_value, "term")
+    summed = jnp.sum(lax.all_gather(partial_value, "term"), axis=0)
     return lax.dynamic_slice_in_dim(summed, lax.axis_index("term") * share, share, 2)
 
 

time: 565 us -> 645 us (1.14)
  the two profiles are of different devices: /device:TPU:2 before, /device:TPU:1 now
where the time goes in v1:
time: 645 us; the launch traced here: 643 us
  waiting for transfers between devices  373 us (58%)
  other arithmetic  103 us (16%)
  local copies, waits for them, and re-layouts  97.5 us (15%)
  matrix products  43 us (7%)
  between operations  13.2 us (2%)
  starting transfers between devices  12.4 us (2%)
    all_gather x1, waiting for transfers between devices, shards(): summed = jnp.sum(lax.all_gather(partial_value, 'term'), axis=0)  177 us
    all_gather x1, waiting for transfers between devices, shards(): lax.all_gather(left_env, 'sector', axis=1, tiled=True)  109 us
    all_to_all x1, waiting for transfers between devices, shards(): lax.all_to_all(outgoing, 'sector', split_axis=0, concat_axis=0, tiled=True)  85.9 us
    scatter-add x11, other arithmetic, step(): return total.at[rows[:, 2]].add(contract(first, second))  81.9 us
    gather x11, local copies, waits for them, and re-layouts, step(): first = jnp.take(first_tiles, rows[:, 0], axis=0)  36.8 us
    dot_general x8, matrix products, right_product(): jnp.einsum('bvij,bjk->bvik', inter_part, env_part, preferred_element_type...  34.6 us
    gather x11, local copies, waits for them, and re-layouts, step(): second = jnp.take(second_tiles, rows[:, 1], axis=0)  31.7 us
    transpose x3, local copies, waits for them, and re-layouts, left_product(): jnp.einsum('bij,bvjk->bvik', env_part, wave_part, preferred_element_type=...  16.8 us
  transfers between devices with their start and end apart: 4, of which 3 were waited for; matrix products, arithmetic and copies ran while one was open for 13% of the time, Pallas kernels for 0%

profile of v1, /device:TPU:1, one launch (start us, length us, event | category | flops | bytes accessed | tf_op | source)
XLA Modules:
  0.0 643.0 jit_solution(10165461063882548504)
XLA Ops:
  8.0 6.5 %gather_fusion.4 = bf16[128,2,128,128]{3,2,1,0:T(8,128)(2,1)} fusion(bf16[16,2,128,128]{3,2,1,0:T(8,128)(2,1)S(1)} %copy-done, s32[1024]{0:T(1024)S(1)} %pad_clamp_fusion.4), kind=kCustom, calls=%fused_computation.4 | custom fusion | bytes 16777728 | tf_op jit(solution)/shard_map/jit(_take)/gather | solution.py:40
  14.5 7.5 %select_select_fusion = bf16[128,2,128,128]{3,2,1,0:T(8,128)(2,1)} fusion(bf16[128,2,128,128]{3,2,1,0:T(8,128)(2,1)} %gather_fusion.4, pred[128]{0:T(512)(128)(4,1)S(1)} %get-tuple-element.225, pred[128]{0:T(512)(128)(4,1)S(1)} %get-tuple-element.224), kind=kLoop, calls=%fused_computation.45 | loop fusion | flops 8388608 | bytes 16777472 | tf_op jit(solution)/shard_map/jit(_where)/select_n | solution.py:41
  22.0 12.1 %all-to-all-start = ((bf16[128,2,128,128]{3,2,1,0:T(8,128)(2,1)}), bf16[128,2,128,128]{3,2,1,0:T(8,128)(2,1)}, u32[]{:S(2)}, u32[]{:S(2)}) async-start(bf16[128,2,128,128]{3,2,1,0:T(8,128)(2,1)} %select_select_fusion), calls=%async_computation | async-start | bytes 16777216 | tf_op jit(solution)/shard_map/all_to_all | solution.py:45
  35.9 109.1 %all-gather.5.cloned.1.call-done = bf16[1,64,128,128]{3,2,0,1:T(8,128)(2,1)} async-done(((bf16[1,1,128,128]{3,2,0,1:T(8,128)(2,1)}), bf16[1,64,128,128]{3,2,0,1:T(8,128)(2,1)}) %all-gather.5.cloned.1.call-update) | async-done | bytes 2097168 | tf_op jit(solution)/shard_map/all_gather | solution.py:33
  145.0 85.9 %all-to-all-done = bf16[128,2,128,128]{3,2,1,0:T(8,128)(2,1)} async-done(((bf16[128,2,128,128]{3,2,1,0:T(8,128)(2,1)}), bf16[128,2,128,128]{3,2,1,0:T(8,128)(2,1)}, u32[]{:S(2)}, u32[]{:S(2)}) %all-to-all-start) | async-done | bytes 8388640 | tf_op jit(solution)/shard_map/all_to_all | solution.py:45
  231.0 2.4 broadcast_in_dim.85
  233.4 75.7 %while.26 = (s32[]{:T(128)}, f32[32,2,128,128]{3,2,1,0:T(8,128)}, s32[96,3]{0,1:T(4,128)S(1)}, bf16[128,2,128,128]{3,2,1,0:T(8,128)(2,1)}, bf16[64,128,128]{2,1,...) while((s32[]{:T(128)}, f32[32,2,128,128]{3,2,1,0:T(8,128)}, s32[96,3]{0,1:T(4,128)S(1)}, ...), condition=%wide.region_2.4_spmd, body=%wide.region_0.3_spmd.sunk | while | flops 271059520 | bytes 34613776 | solution.py:20
  233.5 4.3 gather_fusion
  237.9 2.3 gather_fusion.1
  240.2 2.8 convolution_bitcast_fusion.2
  243.0 5.6 copy.23
  248.7 10.0 %scatter_fusion = f32[32,2,128,128]{3,2,1,0:T(8,128)} fusion(f32[32,2,128,128]{3,2,1,0:T(8,128)} %get-tuple-element.314, s32[32]{0:T(128)S(1)} %get-tuple-element.291, f32[32,2,128,128]{3,2,1,0:T(8,128)} %copy.23), kind=kCustom, calls=%fused_computation.5.clone.1 | custom fusion | flops 1048576 | bytes 12583040 | tf_op jit(solution)/shard_map/while/body/eval_jaxpr/scatter-add | solution.py:18
  258.7 4.3 gather_fusion
  265.4 2.8 convolution_bitcast_fusion.2
  268.2 5.6 copy.23
  273.9 10.1 %scatter_fusion = f32[32,2,128,128]{3,2,1,0:T(8,128)} fusion(f32[32,2,128,128]{3,2,1,0:T(8,128)} %get-tuple-element.314, s32[32]{0:T(128)S(1)} %get-tuple-element.291, f32[32,2,128,128]{3,2,1,0:T(8,128)} %copy.23), kind=kCustom, calls=%fused_computation.5.clone.1 | custom fusion | flops 1048576 | bytes 12583040 | tf_op jit(solution)/shard_map/while/body/eval_jaxpr/scatter-add | solution.py:18
  284.0 4.3 gather_fusion
  290.7 2.8 convolution_bitcast_fusion.2
  293.5 5.6 copy.23
  299.1 10.0 %scatter_fusion = f32[32,2,128,128]{3,2,1,0:T(8,128)} fusion(f32[32,2,128,128]{3,2,1,0:T(8,128)} %get-tuple-element.314, s32[32]{0:T(128)S(1)} %get-tuple-element.291, f32[32,2,128,128]{3,2,1,0:T(8,128)} %copy.23), kind=kCustom, calls=%fused_computation.5.clone.1 | custom fusion | flops 1048576 | bytes 12583040 | tf_op jit(solution)/shard_map/while/body/eval_jaxpr/scatter-add | solution.py:18
  309.1 3.9 convert_element_type.3
  313.3 136.3 %while.27 = (s32[]{:T(128)}, f32[16,2,128,128]{3,2,1,0:T(8,128)S(1)}, s32[256,3]{0,1:T(4,128)S(1)}, bf16[32,2,128,128]{3,2,1,0:T(8,128)(2,1)}, bf16[64,128,128]{...) while((s32[]{:T(128)}, f32[16,2,128,128]{3,2,1,0:T(8,128)S(1)}, ...), condition=%wide.region_5.7_spmd, body=%wide.region_3.6_spmd.sunk | while | flops 271059520 | bytes 26225168 | solution.py:20
  313.4 3.7 gather_fusion.2
  319.5 4.3 fusion.34
  323.8 6.5 %scatter_fusion.1 = f32[16,2,128,128]{3,2,1,0:T(8,128)S(1)} fusion(f32[16,2,128,128]{3,2,1,0:T(8,128)S(1)} %get-tuple-element.341, s32[32]{0:T(128)S(1)} %get-tuple-element.300, f32[32,2,128,128]{3,2,1,0:T(8,128)} %fusion.34), kind=kCustom, calls=%fused_computation.6.clone.1 | custom fusion | flops 1048576 | bytes 12583040 | tf_op jit(solution)/shard_map/while/body/eval_jaxpr/scatter-add | solution.py:18
  330.4 3.7 gather_fusion.2
  336.5 4.3 fusion.34
  340.8 6.5 %scatter_fusion.1 = f32[16,2,128,128]{3,2,1,0:T(8,128)S(1)} fusion(f32[16,2,128,128]{3,2,1,0:T(8,128)S(1)} %get-tuple-element.341, s32[32]{0:T(128)S(1)} %get-tuple-element.300, f32[32,2,128,128]{3,2,1,0:T(8,128)} %fusion.34), kind=kCustom, calls=%fused_computation.6.clone.1 | custom fusion | flops 1048576 | bytes 12583040 | tf_op jit(solution)/shard_map/while/body/eval_jaxpr/scatter-add | solution.py:18
  347.4 3.7 gather_fusion.2
  353.5 4.3 fusion.34
  357.9 6.5 %scatter_fusion.1 = f32[16,2,128,128]{3,2,1,0:T(8,128)S(1)} fusion(f32[16,2,128,128]{3,2,1,0:T(8,128)S(1)} %get-tuple-element.341, s32[32]{0:T(128)S(1)} %get-tuple-element.300, f32[32,2,128,128]{3,2,1,0:T(8,128)} %fusion.34), kind=kCustom, calls=%fused_computation.6.clone.1 | custom fusion | flops 1048576 | bytes 12583040 | tf_op jit(solution)/shard_map/while/body/eval_jaxpr/scatter-add | solution.py:18
  364.5 3.7 gather_fusion.2
  370.6 4.3 fusion.34
  374.9 6.5 %scatter_fusion.1 = f32[16,2,128,128]{3,2,1,0:T(8,128)S(1)} fusion(f32[16,2,128,128]{3,2,1,0:T(8,128)S(1)} %get-tuple-element.341, s32[32]{0:T(128)S(1)} %get-tuple-element.300, f32[32,2,128,128]{3,2,1,0:T(8,128)} %fusion.34), kind=kCustom, calls=%fused_computation.6.clone.1 | custom fusion | flops 1048576 | bytes 12583040 | tf_op jit(solution)/shard_map/while/body/eval_jaxpr/scatter-add | solution.py:18
  381.5 3.7 gather_fusion.2
  387.6 4.3 fusion.34
  391.9 6.5 %scatter_fusion.1 = f32[16,2,128,128]{3,2,1,0:T(8,128)S(1)} fusion(f32[16,2,128,128]{3,2,1,0:T(8,128)S(1)} %get-tuple-element.341, s32[32]{0:T(128)S(1)} %get-tuple-element.300, f32[32,2,128,128]{3,2,1,0:T(8,128)} %fusion.34), kind=kCustom, calls=%fused_computation.6.clone.1 | custom fusion | flops 1048576 | bytes 12583040 | tf_op jit(solution)/shard_map/while/body/eval_jaxpr/scatter-add | solution.py:18
  398.5 3.7 gather_fusion.2
  404.6 4.3 fusion.34
  409.0 6.5 %scatter_fusion.1 = f32[16,2,128,128]{3,2,1,0:T(8,128)S(1)} fusion(f32[16,2,128,128]{3,2,1,0:T(8,128)S(1)} %get-tuple-element.341, s32[32]{0:T(128)S(1)} %get-tuple-element.300, f32[32,2,128,128]{3,2,1,0:T(8,128)} %fusion.34), kind=kCustom, calls=%fused_computation.6.clone.1 | custom fusion | flops 1048576 | bytes 12583040 | tf_op jit(solution)/shard_map/while/body/eval_jaxpr/scatter-add | solution.py:18
  415.6 3.7 gather_fusion.2
  421.7 4.3 fusion.34
  426.0 6.5 %scatter_fusion.1 = f32[16,2,128,128]{3,2,1,0:T(8,128)S(1)} fusion(f32[16,2,128,128]{3,2,1,0:T(8,128)S(1)} %get-tuple-element.341, s32[32]{0:T(128)S(1)} %get-tuple-element.300, f32[32,2,128,128]{3,2,1,0:T(8,128)} %fusion.34), kind=kCustom, calls=%fused_computation.6.clone.1 | custom fusion | flops 1048576 | bytes 12583040 | tf_op jit(solution)/shard_map/while/body/eval_jaxpr/scatter-add | solution.py:18
  432.6 3.7 gather_fusion.2
  438.7 4.3 fusion.34
  443.0 6.5 %scatter_fusion.1 = f32[16,2,128,128]{3,2,1,0:T(8,128)S(1)} fusion(f32[16,2,128,128]{3,2,1,0:T(8,128)S(1)} %get-tuple-element.341, s32[32]{0:T(128)S(1)} %get-tuple-element.300, f32[32,2,128,128]{3,2,1,0:T(8,128)} %fusion.34), kind=kCustom, calls=%fused_computation.6.clone.1 | custom fusion | flops 1048576 | bytes 12583040 | tf_op jit(solution)/shard_map/while/body/eval_jaxpr/scatter-add | solution.py:18
  450.9 176.9 %all-gather.9.cloned.1.call-done = f32[128,2,128,128]{3,2,1,0:T(8,128)} async-done(((f32[16,2,128,128]{3,2,1,0:T(8,128)}), f32[128,2,128,128]{3,2,1,0:T(8,128)}) %all-gather.9.cloned.1.call-update) | async-done | bytes 16777232 | tf_op jit(solution)/shard_map/all_gather | solution.py:52
  627.8 7.9 %reduce_sum.9 = f32[16,2,128,128]{3,2,1,0:T(8,128)S(1)} reduce(f32[8,16,2,128,128]{4,3,2,1,0:T(8,128)} %bitcast.61, f32[]{:T(128)} %constant.155.clone.1), dimensions={0}, to_apply=%region_6.8 | reduce | flops 3670016 | bytes 18874372 | tf_op jit(solution)/shard_map/reduce_sum | solution.py:52
  (100 shorter events, 30.1 us)
Async XLA Ops:
  6.5 1.4 copy-start
  22.0 13.9 %copy-start.4 = (s32[1,1,96,3]{2,1,3,0:T(1,128)S(1)}, s32[1,1,96,3]{2,1,3,0:T(1,128)}, u32[]{:S(2)}) copy-start(s32[1,1,96,3]{2,1,3,0:T(1,128)} %param.16) | copy-start | bytes 3460
  22.0 13.9 %copy-start.3 = (s32[1,1,256,3]{2,1,3,0:T(1,128)S(1)}, s32[1,1,256,3]{2,1,3,0:T(1,128)}, u32[]{:S(2)}) copy-start(s32[1,1,256,3]{2,1,3,0:T(1,128)} %param.17) | copy-start | bytes 9220
  22.0 208.9 %all-to-all-start = ((bf16[128,2,128,128]{3,2,1,0:T(8,128)(2,1)}), bf16[128,2,128,128]{3,2,1,0:T(8,128)(2,1)}, u32[]{:S(2)}, u32[]{:S(2)}) async-start(bf16[128,2,128,128]{3,2,1,0:T(8,128)(2,1)} %select_select_fusion), calls=%async_computation | async-start | bytes 16777216 | tf_op jit(solution)/shard_map/all_to_all | solution.py:45
  34.1 110.9 %all-gather.5.cloned.1.call-start = ((), (), s32[]{:S(2)}) async-start(), calls=%async_computation.1 | async-start | bytes 2129920 | tf_op jit(solution)/shard_map/all_gather | solution.py:33
  34.9 278.2 %all-gather.7.cloned.1.call-start = ((), (), s32[]{:S(2)}) async-start(), calls=%async_computation.2 | async-start | bytes 2129920 | tf_op jit(solution)/shard_map/all_gather | solution.py:34
  35.6 592.2 %all-gather.9.cloned.1.call-start = ((), (), s32[]{:S(2)}) async-start(), calls=%async_computation.3 | async-start | bytes 18874368 | tf_op jit(solution)/shard_map/all_gather | solution.py:52
  449.5 1.3 copy-start.2
  627.8 8.6 %copy-start.1 = (bf16[16,2,128,128]{3,2,1,0:T(8,128)(2,1)S(1)}, bf16[16,2,128,128]{3,2,1,0:T(8,128)(2,1)}, u32[]{:S(2)}) copy-start(bf16[16,2,128,128]{3,2,1,0:T(8,128)(2,1)} %param.12) | copy-start | bytes 3145732
Sparse Core Ops, SparseCore 0:
  38.3 106.6 all-gather.4
  148.4 89.1 all-gather.6
  451.0 176.7 all-gather.8
